TPU v7x, 32 devices: a whole 2x2x4 slice. The times are simulated.
32 devices in a mesh: ctx: 2 (over y), ch: 16 (over z, x, core).
Axes of the slice: x: 2, y: 2, z: 4, core: 2. Of those that a mesh axis runs over, the one named last changes fastest.
Arguments:
- projections: bfloat16 [4, 1024, 3, 4096], P(None, ('ctx', 'ch')), may hold values from -6 to 6
- impulse: float32 [1024, 4096], P('ctx', 'ch'), may hold values from -4 to 4, as said below
- skip_gain: float32 [4096], P('ch'), may hold values from 0.3 to 1.5
Outputs:
- gated: bfloat16 [4, 1024, 4096], P(None, ('ctx', 'ch'))
Inputs may be any that keep to these rules, and one draw needn't show every extreme that they name: impulse holds a filter of each channel over lags.
All inputs are finite; a program needn't handle non-finite values.
Results may differ from a plain program's by a relative error of at most 0.0056.
Values may be sent and summed in bfloat16 or wider, within the bound.
A program may use at most 128 MiB of HBM per device.

v0:
```python
import math
import jax
import jax.numpy as jnp
from jax import lax
from jax.sharding import PartitionSpec as P


def passed_along(value, axis, steps):
    count = lax.axis_size(axis)
    leading, last = (max(0, -steps), min(count, count - steps))
    return lax.ppermute(value, axis, [(source, source + steps) for source in range(leading, last)])


def forward_table(length):
    frequency = lax.broadcasted_iota(jnp.int32, (length, length), 0)
    sample = lax.broadcasted_iota(jnp.int32, (length, length), 1)
    angles = (frequency * sample % (2 * length)).astype(jnp.float32) * (math.pi / length)
    nyquist = jnp.where(sample % 2 == 0, jnp.float32(1.0), jnp.float32(-1.0))
    packed_imag = jnp.where(frequency == 0, nyquist, -jnp.sin(angles))
    return jnp.stack([jnp.cos(angles), packed_imag], axis=0)


def inverse_table(length):
    sample = lax.broadcasted_iota(jnp.int32, (2 * length, length), 0)
    frequency = lax.broadcasted_iota(jnp.int32, (2 * length, length), 1)
    angles = (frequency * sample % (2 * length)).astype(jnp.float32) * (math.pi / length)
    weight = jnp.where(frequency == 0, jnp.float32(0.5), jnp.float32(1.0)) / length
    nyquist = jnp.where(sample % 2 == 0, jnp.float32(0.5), jnp.float32(-0.5)) / length
    imag_part = jnp.where(frequency == 0, nyquist, -weight * jnp.sin(angles))
    return jnp.stack([weight * jnp.cos(angles), imag_part], axis=1)


def spectral_product(left_side, right_side):
    left_real = left_side[..., 0, :, :]
    left_imag = left_side[..., 1, :, :]
    right_real = right_side[..., 0, :, :]
    right_imag = right_side[..., 1, :, :]
    first_bin = lax.broadcasted_iota(jnp.int32, (left_real.shape[-2], 1), 0) == 0
    real_part = jnp.where(
        first_bin, left_real * right_real, left_real * right_real - left_imag * right_imag
    )
    imag_part = jnp.where(
        first_bin, left_imag * right_imag, left_real * right_imag + left_imag * right_real
    )
    return jnp.stack([real_part, imag_part], axis=-3)


def body(projections, impulse, skip_gain):
    length = impulse.shape[0]
    blocks = lax.axis_size("ctx")
    position = lax.axis_index("ctx")
    forward = forward_table(length)
    forward_low = forward.astype(jnp.bfloat16)
    received = lax.all_to_all(projections, "ch", split_axis=3, concat_axis=1, tiled=True)
    gate_part = received[:, :, 0, :]
    mixed_input = (
        received[:, :, 1, :].astype(jnp.float32) * received[:, :, 2, :].astype(jnp.float32)
    ).astype(jnp.bfloat16)
    spectrum, mixed_input, gate_rows = (
        jnp.einsum(
            "pkn,snc->spkc", forward_low, mixed_input, preferred_element_type=jnp.float32
        ).astype(jnp.bfloat16),
        mixed_input,
        gate_part,
    )
    own_filter = jnp.einsum("pkn,nc->pkc", forward, impulse, precision=lax.Precision.HIGHEST)
    filters = lax.all_gather(own_filter[None], "ctx", axis=0, tiled=True)
    zero_carry = jnp.zeros(spectrum.shape, jnp.float32)
    pieces = lax.all_gather(spectrum[None], "ctx", axis=0, tiled=True)
    current = zero_carry
    previous = zero_carry
    for offset in range(pieces.shape[0]):
        source = pieces[offset].astype(jnp.float32)
        lag_index = position - offset
        chosen = lax.dynamic_index_in_dim(
            filters, jnp.clip(lag_index, 0, blocks - 1), 0, keepdims=False
        )
        weight = (lag_index >= 0).astype(jnp.float32)
        current = current + spectral_product(source, chosen) * weight
    current, previous = (current, previous)
    inverse = inverse_table(length)
    signal = jnp.einsum("npk,spkc->snc", inverse, current, precision=lax.Precision.HIGHEST)
    head_part = signal[:, :length]
    tail_part = passed_along(signal[:, length:], "ctx", 1)
    mixed_wide = lax.optimization_barrier(mixed_input).astype(jnp.float32)
    convolved = head_part + tail_part + skip_gain * mixed_wide
    gated = (gate_rows.astype(jnp.float32) * convolved).astype(jnp.bfloat16)
    return lax.all_to_all(gated, "ch", split_axis=1, concat_axis=2, tiled=True)


def solution(mesh):
    return jax.shard_map(
        body,
        mesh=mesh,
        in_specs=(P(None, ("ctx", "ch"), None, None), P("ctx", "ch"), P("ch")),
        out_specs=P(None, ("ctx", "ch"), None),
        check_vma=False,
    )
```

profile of v0, /device:TPU:13, one launch (start us, length us, event | category | flops | bytes accessed | tf_op | source)
XLA Modules:
  0.0 349.7 jit_solution(7590995391529949051)
XLA Ops:
  6.5 0.0 copy-start
  6.5 16.6 %copy.33 = bf16[4,32,3,4096]{1,0,2,3:T(4,128)(2,1)} copy(bf16[4,32,3,4096]{3,1,2,0:T(8,128)(2,1)} %param.3) | data formatting | bytes 6291456 | tf_op args[0]
  23.1 17.7 %reshape.390 = bf16[16,2,49152]{2,1,0:T(2,128)(2,1)} reshape(bf16[4096,3,4,32]{3,2,1,0:T(4,128)(2,1)} %bitcast.50) | data formatting | bytes 6291456
  40.8 6.6 %all-to-all-start = ((bf16[16,2,49152]{2,1,0:T(2,128)(2,1)}), bf16[16,2,49152]{2,1,0:T(2,128)(2,1)}, u32[]{:S(2)}, u32[]{:S(2)}) async-start(bf16[16,2,49152]{2,1,0:T(2,128)(2,1)} %reshape.390), calls=%async_computation | async-start | bytes 6291456 | tf_op jit(solution)/shard_map/all_to_all | solution.py:54
  47.4 0.0 all-gather.7.cloned.1.call-start
  47.4 3.8 %fusion.35 = f32[1,512,512]{2,1,0:T(8,128)S(1)} fusion(), kind=kLoop, calls=%fused_computation.61 | loop fusion | flops 3670016 | bytes 1048576 | tf_op jit(solution)/shard_map/cos | solution.py:20
  51.2 0.0 copy-start.2
  51.2 4.0 %negate_select_fusion.4 = f32[1,512,512]{2,1,0:T(8,128)S(1)} fusion(s32[512]{0:T(512)S(1)} %get-tuple-element.22, s32[512]{0:T(512)S(1)} %get-tuple-element.23, pred[512]{0:T(512)(128)(4,1)S(1)} %get-tuple-element.24, pred[512]{0:T(512)(128)(4,1)S(1)} %get-tuple-element.25), kind=kLoop, calls=%fused_computation.51 | loop fusion | flops 4980736 | bytes 1053696 | tf_op jit(solution)/shard_map/jit(_where)/select_n | solution.py:19
  55.2 0.0 copy-done.2
  55.2 0.0 copy-start.3
  55.2 1.0 copy-done.3
  56.2 0.0 copy-done
  56.2 2.8 fusion.23
  59.0 0.0 all-gather.7.cloned.1.call-update
  59.0 0.2 all-gather.5.cloned.1.call-start
  59.3 55.9 %all-to-all-done = bf16[16,2,49152]{2,1,0:T(2,128)(2,1)} async-done(((bf16[16,2,49152]{2,1,0:T(2,128)(2,1)}), bf16[16,2,49152]{2,1,0:T(2,128)(2,1)}, u32[]{:S(2)}, u32[]{:S(2)}) %all-to-all-start) | async-done | bytes 3145760 | tf_op jit(solution)/shard_map/all_to_all | solution.py:54
  115.2 14.5 %reshape.391 = bf16[4096,3,4,32]{3,2,1,0:T(4,128)(2,1)} reshape(bf16[16,2,49152]{2,1,0:T(2,128)(2,1)} %all-to-all-done) | data formatting | bytes 6291456
  129.7 17.7 %copy.48 = bf16[4,32,3,16,256]{4,1,3,2,0:T(8,128)(2,1)} copy(bf16[4,32,3,16,256]{1,0,2,4,3:T(4,128)(2,1)} %bitcast.49) | data formatting | bytes 6291456 | tf_op jit(solution)/shard_map/all_to_all | solution.py:54
  147.4 3.4 fusion.49
  150.8 0.5 copy.50
  151.3 1.5 copy.51
  152.8 4.2 %convert_bitcast_fusion = bf16[4,2,512,256]{2,3,1,0:T(8,128)(2,1)} fusion(f32[1,512,512]{2,1,0:T(8,128)} %copy-done.3, f32[1,512,512]{2,1,0:T(8,128)} %copy-done.2, bf16[4,512,1,256]{1,3,0,2:T(8,128)(2,1)S(1)} %copy.51, bf16[4,512,1,256]{1,3,0,2:T(8,128)(2,1)S(1)} %copy.50), kind=kOutput, calls=%fused_computation.36 | convolution fusion | flops 1078984704 | bytes 6291456 | tf_op jit(solution)/shard_map/pkn,snc->spkc/dot_general | solution.py:60
  157.0 4.2 %copy.39 = bf16[4,2,512,256]{3,2,1,0:T(8,128)(2,1)} copy(bf16[4,2,512,256]{2,3,1,0:T(8,128)(2,1)} %convert_bitcast_fusion) | data formatting | bytes 4194304 | tf_op jit(solution)/shard_map/convert_element_type | solution.py:62
  161.2 0.0 all-gather.5.cloned.1.call-update
  161.3 8.6 %cosine_multiply_fusion = f32[1024,1,512]{2,0,1:T(8,128)} fusion(f32[512]{0:T(512)S(1)} %select_multiply_fusion), kind=kLoop, calls=%fused_computation.29 | loop fusion | flops 7864320 | bytes 2099200 | tf_op jit(solution)/shard_map/mul | solution.py:30
  169.9 9.0 %multiply_select_fusion = f32[1024,1,512]{2,0,1:T(8,128)} fusion(f32[512]{0:T(512)S(1)} %fusion.45, s32[1024]{0:T(1024)S(1)} %get-tuple-element.20, s32[1024]{0:T(1024)S(1)} %get-tuple-element.21, pred[1024]{0:T(1024)(128)(4,1)S(1)} %fusion.40, pred[512]{0:T(512)(128)(4,1)S(1)} %get-tuple-element.24), kind=kLoop, calls=%fused_computation.27 | loop fusion | flops 10485760 | bytes 2108928 | tf_op jit(solution)/shard_map/jit(_where)/select_n | solution.py:29
  178.9 0.0 all-gather.7.cloned.1.call-done
  178.9 2.7 dynamic-slice_bitcast_fusion.1
  181.6 37.2 %all-gather.5.cloned.1.call-done = bf16[8,2,512,256]{3,2,1,0:T(8,128)(2,1)} async-done(((bf16[4,2,512,256]{3,2,1,0:T(8,128)(2,1)}), bf16[8,2,512,256]{3,2,1,0:T(8,128)(2,1)}) %all-gather.5.cloned.1.call-update) | async-done | bytes 4194320 | tf_op jit(solution)/shard_map/all_gather | solution.py:69
  218.8 0.0 copy-start.6
  218.8 0.0 copy-start.7
  218.8 3.2 slice_convert_fusion
  222.0 0.0 copy-done.6
  222.0 0.0 copy-done.7
  222.0 0.0 copy-start.8
  222.0 0.0 copy-start.9
  222.0 1.4 subtract_select_fusion
  223.5 0.1 copy-done.8
  223.6 0.6 copy-done.9
  224.3 27.5 %fusion.9 = f32[4,1024,256]{1,2,0:T(8,128)S(1)} fusion(f32[1024,1,512]{2,0,1:T(8,128)S(1)} %copy-done.8, f32[1024,1,512]{2,0,1:T(8,128)S(1)} %copy-done.9, f32[4,1,512,256]{3,2,1,0:T(8,128)S(1)} %get-tuple-element.18, f32[4,1,512,256]{3,2,1,0:T(8,128)S(1)} %get-tuple-element.19, f32[4,1,512,256]{3,2,1,0:T(8,128)S(1)} %get-tuple-element.6, ...), kind=kOutput, calls=%fused_computation.16 | convolution fusion | flops 12891193344 | bytes 16777224 | tf_op jit(solution)/shard_map/npk,spkc->snc/dot_general | solution.py:82
  251.8 0.0 copy-start.5
  251.8 1.7 slice.76
  253.5 1.0 copy-done.5
  254.5 0.0 copy-start.10
  254.5 1.4 collective-permute-start
  255.9 1.3 fusion.36
  257.2 0.0 copy-start.4
  257.2 1.6 copy.49
  258.8 44.5 %collective-permute-done = f32[4,512,256]{1,2,0:T(8,128)} collective-permute-done((f32[4,512,256]{1,2,0:T(8,128)}, f32[4,512,256]{1,2,0:T(8,128)}, u32[]{:S(2)}, u32[]{:S(2)}) %collective-permute-start) | collective-permute-done | bytes 2097184 | tf_op jit(solution)/shard_map/ppermute | solution.py:11
  303.3 0.0 copy-done.10
  303.3 0.0 copy-done.4
  303.3 4.0 %fusion.17 = bf16[4,512,256]{1,2,0:T(8,128)(2,1)} fusion(f32[4,512,256]{1,2,0:T(8,128)} %collective-permute-done, f32[4,1024,256]{1,2,0:T(8,128)} %copy-done.5, bf16[4,512,256]{1,2,0:T(8,128)(2,1)S(1)} %copy-done.4, bf16[4,512,1,256]{1,3,0,2:T(8,128)(2,1)S(1)} %copy.49, f32[256]{0:T(256)S(1)} %copy-done.10), kind=kLoop, calls=%fused_computation.23 | loop fusion | flops 3670016 | bytes 7341056 | tf_op jit(solution)/shard_map/convert_element_type | solution.py:87
  307.3 1.7 copy.41
  309.0 0.0 copy-start.1
  309.0 32.6 %all_to_all.36 = bf16[4,512,256]{2,0,1:T(4,128)(2,1)S(1)} all-to-all(bf16[4,512,256]{2,0,1:T(4,128)(2,1)S(1)} %copy.41), channel_id=1, replica_groups=mesh['ctx'=2,'ch'=16] {'ch'}, dimensions={1} | all-to-all | bytes 2097152 | tf_op jit(solution)/shard_map/all_to_all | solution.py:88
  341.6 0.1 copy.42
  341.8 1.1 copy.52
  342.9 0.0 copy-done.1
  (6 shorter events, 0.0 us)
Async XLA Ops:
  6.5 49.7 %copy-start = (f32[512,256]{1,0:T(8,128)S(1)}, f32[512,256]{1,0:T(8,128)}, u32[]{:S(2)}) copy-start(f32[512,256]{1,0:T(8,128)} %param.4) | copy-start | bytes 1572868
  40.8 74.4 %all-to-all-start = ((bf16[16,2,49152]{2,1,0:T(2,128)(2,1)}), bf16[16,2,49152]{2,1,0:T(2,128)(2,1)}, u32[]{:S(2)}, u32[]{:S(2)}) async-start(bf16[16,2,49152]{2,1,0:T(2,128)(2,1)} %reshape.390), calls=%async_computation | async-start | bytes 6291456 | tf_op jit(solution)/shard_map/all_to_all | solution.py:54
  47.4 131.6 %all-gather.7.cloned.1.call-start = ((), (), s32[]{:S(2)}) async-start(), calls=%async_computation.3 | async-start | bytes 3145728 | tf_op jit(solution)/shard_map/all_gather | solution.py:67
  51.2 4.0 %copy-start.2 = (f32[1,512,512]{2,1,0:T(8,128)}, f32[1,512,512]{2,1,0:T(8,128)S(1)}, u32[]{:S(2)}) copy-start(f32[1,512,512]{2,1,0:T(8,128)S(1)} %fusion.35) | copy-start | bytes 3145732
  55.2 1.0 copy-start.3
  59.0 159.8 %all-gather.5.cloned.1.call-start = ((), (), s32[]{:S(2)}) async-start(), calls=%async_computation.2 | async-start | bytes 6291456 | tf_op jit(solution)/shard_map/all_gather | solution.py:69
  218.8 3.2 copy-start.6
  218.8 3.2 copy-start.7
  222.0 1.6 copy-start.8
  222.0 2.2 copy-start.9
  251.8 2.7 copy-start.5
  254.5 48.8 %copy-start.10 = (f32[256]{0:T(256)S(1)}, f32[256]{0:T(256)}, u32[]{:S(2)}) copy-start(f32[256]{0:T(256)} %param.5) | copy-start | bytes 3076
  254.5 48.8 %collective-permute-start = (f32[4,512,256]{1,2,0:T(8,128)}, f32[4,512,256]{1,2,0:T(8,128)}, u32[]{:S(2)}, u32[]{:S(2)}) collective-permute-start(f32[4,512,256]{1,2,0:T(8,128)} %slice.76), channel_id=1, source_target_pairs={{0,16},{1,17},{2,18},{3,19},{4,20},{5,21},{6,22},{7,23},{8,24},{9,... | collective-permute-start | bytes 6291464 | tf_op jit(solution)/shard_map/ppermute | solution.py:11
  257.2 46.1 %copy-start.4 = (bf16[4,512,256]{1,2,0:T(8,128)(2,1)S(1)}, bf16[4,512,256]{1,2,0:T(8,128)(2,1)}, u32[]{:S(2)}) copy-start(bf16[4,512,256]{1,2,0:T(8,128)(2,1)} %fusion.36) | copy-start | bytes 3145732
  309.0 33.9 %copy-start.1 = (f32[512,256]{1,0:T(8,128)S(1)}, f32[512,256]{1,0:T(8,128)}, u32[]{:S(2)}) copy-start(f32[512,256]{1,0:T(8,128)} %param.4) | copy-start | bytes 1572868
Sparse Core Ops, SparseCore 0:
  59.1 32.7 all-gather.6
  161.3 57.4 all-gather.4
where the time goes:
time: 352 us; the launch traced here: 350 us
  waiting for transfers between devices  138 us (39%)
  local copies, waits for them, and re-layouts  87.6 us (25%)
  other arithmetic  35.4 us (10%)
  matrix products  34.5 us (10%)
  blocking collectives  32.6 us (9%)
  between operations  13.6 us (4%)
  starting transfers between devices  8.25 us (2%)
    all_to_all x1, waiting for transfers between devices, body(): lax.all_to_all(projections, 'ch', split_axis=3, concat_axis=1, tiled=True)  55.9 us
    unnamed x28, local copies, waits for them, and re-layouts  55.1 us
    ppermute x1, waiting for transfers between devices, passed_along(): lax.ppermute(value, axis, [(source, source + steps) for source in range(l...  44.5 us
    all_gather x1, waiting for transfers between devices, body(): pieces = lax.all_gather(spectrum[None], 'ctx', axis=0, tiled=True)  37.2 us
    all_to_all x1, blocking collectives, body(): return lax.all_to_all(gated, 'ch', split_axis=1, concat_axis=2, tiled=True)  32.6 us
    dot_general x1, matrix products, body(): jnp.einsum('npk,spkc->snc', inverse, current, precision=lax.Precision.HIG...  27.5 us
    all_to_all x1, local copies, waits for them, and re-layouts, body(): lax.all_to_all(projections, 'ch', split_axis=3, concat_axis=1, tiled=True)  17.7 us
    select_n x1, other arithmetic, inverse_table(): imag_part = jnp.where(frequency == 0, nyquist, -weight * jnp.sin(angles))  9 us
  transfers between devices with their start and end apart: 4, of which 3 were waited for; matrix products, arithmetic and copies ran while one was open for 23% of the time, Pallas kernels for 0%

commit v1 on v0

--- a/solution.py
+++ b/solution.py
@@ -51,7 +51,10 @@
     position = lax.axis_index("ctx")
     forward = forward_table(length)
     forward_low = forward.astype(jnp.bfloat16)
-    received = lax.all_to_all(projections, "ch", split_axis=3, concat_axis=1, tiled=True)
+    received = jnp.concatenate(
+        lax.all_to_all(jnp.stack(jnp.split(projections, lax.axis_size("ch"), axis=3)), "ch", 0, 0),
+        axis=1,
+    )
     gate_part = received[:, :, 0, :]
     mixed_input = (
         received[:, :, 1, :].astype(jnp.float32) * received[:, :, 2, :].astype(jnp.float32)

time: 352 us -> 311 us (0.88)
  local copies, waits for them, and re-layouts: 87.6 us -> 47.8 us
    unnamed x28 -> x40, local copies, waits for them, and re-layouts: 55.1 us -> 30.8 us
    all_to_all x1, local copies, waits for them, and re-layouts: 17.7 us -> 2.32 us  [body(): lax.all_to_all(jnp.stack(jnp.split(projections, lax.axis_size('ch'), axis...]
  transfers between devices with their start and end apart: 4 -> 4, of which waited for: 3 -> 3; matrix products, arithmetic and copies ran while one was open for 23% -> 16% of each run, Pallas kernels for 0% -> 0%
where the time goes in v1:
time: 311 us; the launch traced here: 310 us
  waiting for transfers between devices  138 us (44%)
  local copies, waits for them, and re-layouts  47.8 us (15%)
  other arithmetic  35.4 us (11%)
  matrix products  34.5 us (11%)
  blocking collectives  32.6 us (10%)
  between operations  13.6 us (4%)
  starting transfers between devices  8.25 us (3%)
    all_to_all x1, waiting for transfers between devices, body(): lax.all_to_all(jnp.stack(jnp.split(projections, lax.axis_size('ch'), axis...  56 us
    ppermute x1, waiting for transfers between devices, passed_along(): lax.ppermute(value, axis, [(source, source + steps) for source in range(l...  44.5 us
    all_gather x1, waiting for transfers between devices, body(): pieces = lax.all_gather(spectrum[None], 'ctx', axis=0, tiled=True)  37.2 us
    all_to_all x1, blocking collectives, body(): return lax.all_to_all(gated, 'ch', split_axis=1, concat_axis=2, tiled=True)  32.6 us
    unnamed x40, local copies, waits for them, and re-layouts  30.8 us
    dot_general x1, matrix products, body(): jnp.einsum('npk,spkc->snc', inverse, current, precision=lax.Precision.HIG...  27.5 us
    select_n x1, other arithmetic, inverse_table(): imag_part = jnp.where(frequency == 0, nyquist, -weight * jnp.sin(angles))  8.99 us
    mul x1, other arithmetic, inverse_table(): return jnp.stack([weight * jnp.cos(angles), imag_part], axis=1)  8.63 us
  transfers between devices with their start and end apart: 4, of which 3 were waited for; matrix products, arithmetic and copies ran while one was open for 16% of the time, Pallas kernels for 0%

profile of v1, /device:TPU:13, one launch (start us, length us, event | category | flops | bytes accessed | tf_op | source)
XLA Modules:
  0.0 309.9 jit_solution(12628392263960245045)
XLA Ops:
  6.5 0.0 copy-start
  6.5 1.7 bitcast_dynamic-update-slice_fusion.15
  8.2 1.6 bitcast_dynamic-update-slice_fusion.14
  9.8 1.6 bitcast_dynamic-update-slice_fusion.13
  11.5 1.6 bitcast_dynamic-update-slice_fusion.12
  13.1 1.6 bitcast_dynamic-update-slice_fusion.11
  14.7 1.6 bitcast_dynamic-update-slice_fusion.10
  16.3 1.6 bitcast_dynamic-update-slice_fusion.9
  17.9 1.6 bitcast_dynamic-update-slice_fusion.8
  19.6 1.6 bitcast_dynamic-update-slice_fusion.7
  21.2 1.6 bitcast_dynamic-update-slice_fusion.6
  22.8 1.6 bitcast_dynamic-update-slice_fusion.5
  24.4 1.6 bitcast_dynamic-update-slice_fusion.4
  26.1 1.6 bitcast_dynamic-update-slice_fusion.3
  27.7 1.6 bitcast_dynamic-update-slice_fusion.2
  29.3 1.6 bitcast_dynamic-update-slice_fusion.1
  30.9 1.6 bitcast_dynamic-update-slice_fusion
  32.5 6.6 %all-to-all-start = ((bf16[16,4,32,3,256]{4,2,3,1,0:T(8,128)(2,1)}), bf16[16,4,32,3,256]{4,2,3,1,0:T(8,128)(2,1)}, u32[]{:S(2)}, u32[]{:S(2)}) async-start(bf16[16,4,32,3,256]{4,2,3,1,0:T(8,128)(2,1)} %bitcast_dynamic-update-slice_fusion), calls=%async_computation | async-start | bytes 6291456 | tf_op jit(solution)/shard_map/all_to_all | solution.py:55
  39.1 0.0 all-gather.7.cloned.1.call-start
  39.2 3.8 %fusion.35 = f32[1,512,512]{2,1,0:T(8,128)S(1)} fusion(), kind=kLoop, calls=%fused_computation.61 | loop fusion | flops 3670016 | bytes 1048576 | tf_op jit(solution)/shard_map/cos | solution.py:20
  43.0 0.0 copy-start.2
  43.0 4.0 %negate_select_fusion.4 = f32[1,512,512]{2,1,0:T(8,128)S(1)} fusion(s32[512]{0:T(512)S(1)} %get-tuple-element.22, s32[512]{0:T(512)S(1)} %get-tuple-element.23, pred[512]{0:T(512)(128)(4,1)S(1)} %get-tuple-element.24, pred[512]{0:T(512)(128)(4,1)S(1)} %get-tuple-element.25), kind=kLoop, calls=%fused_computation.51 | loop fusion | flops 4980736 | bytes 1053696 | tf_op jit(solution)/shard_map/jit(_where)/select_n | solution.py:19
  47.0 0.0 copy-done.2
  47.0 0.0 copy-start.3
  47.0 1.0 copy-done.3
  48.0 0.0 copy-done
  48.0 2.8 fusion.23
  50.8 0.0 all-gather.7.cloned.1.call-update
  50.8 0.2 all-gather.5.cloned.1.call-start
  51.0 56.0 %all-to-all-done = bf16[16,4,32,3,256]{4,2,3,1,0:T(8,128)(2,1)} async-done(((bf16[16,4,32,3,256]{4,2,3,1,0:T(8,128)(2,1)}), bf16[16,4,32,3,256]{4,2,3,1,0:T(8,128)(2,1)}, u32[]{:S(2)}, u32[]{:S(2)}) %all-to-all-start) | async-done | bytes 3145760 | tf_op jit(solution)/shard_map/all_to_all | solution.py:55
  107.0 2.3 copy.21
  109.3 1.6 fusion.49
  110.9 0.5 copy.34
  111.4 1.5 copy.35
  112.9 4.2 %convert_bitcast_fusion = bf16[4,2,512,256]{2,3,1,0:T(8,128)(2,1)} fusion(f32[1,512,512]{2,1,0:T(8,128)} %copy-done.3, f32[1,512,512]{2,1,0:T(8,128)} %copy-done.2, bf16[4,512,1,256]{1,3,0,2:T(8,128)(2,1)S(1)} %copy.35, bf16[4,512,1,256]{1,3,0,2:T(8,128)(2,1)S(1)} %copy.34), kind=kOutput, calls=%fused_computation.36 | convolution fusion | flops 1078984704 | bytes 6291456 | tf_op jit(solution)/shard_map/pkn,snc->spkc/dot_general | solution.py:63
  117.1 4.2 %copy.25 = bf16[4,2,512,256]{3,2,1,0:T(8,128)(2,1)} copy(bf16[4,2,512,256]{2,3,1,0:T(8,128)(2,1)} %convert_bitcast_fusion) | data formatting | bytes 4194304 | tf_op jit(solution)/shard_map/convert_element_type | solution.py:65
  121.3 0.0 all-gather.5.cloned.1.call-update
  121.4 8.6 %cosine_multiply_fusion = f32[1024,1,512]{2,0,1:T(8,128)} fusion(f32[512]{0:T(512)S(1)} %select_multiply_fusion), kind=kLoop, calls=%fused_computation.29 | loop fusion | flops 7864320 | bytes 2099200 | tf_op jit(solution)/shard_map/mul | solution.py:30
  130.0 9.0 %multiply_select_fusion = f32[1024,1,512]{2,0,1:T(8,128)} fusion(f32[512]{0:T(512)S(1)} %fusion.45, s32[1024]{0:T(1024)S(1)} %get-tuple-element.20, s32[1024]{0:T(1024)S(1)} %get-tuple-element.21, pred[1024]{0:T(1024)(128)(4,1)S(1)} %fusion.40, pred[512]{0:T(512)(128)(4,1)S(1)} %get-tuple-element.24), kind=kLoop, calls=%fused_computation.27 | loop fusion | flops 10485760 | bytes 2108928 | tf_op jit(solution)/shard_map/jit(_where)/select_n | solution.py:29
  139.0 2.7 dynamic-slice_bitcast_fusion.1
  141.7 37.2 %all-gather.5.cloned.1.call-done = bf16[8,2,512,256]{3,2,1,0:T(8,128)(2,1)} async-done(((bf16[4,2,512,256]{3,2,1,0:T(8,128)(2,1)}), bf16[8,2,512,256]{3,2,1,0:T(8,128)(2,1)}) %all-gather.5.cloned.1.call-update) | async-done | bytes 4194320 | tf_op jit(solution)/shard_map/all_gather | solution.py:72
  178.9 3.2 %slice_convert_fusion = (f32[4,2,512,256]{3,2,1,0:T(8,128)S(1)}, f32[4,2,512,256]{3,2,1,0:T(8,128)S(1)}) fusion(bf16[8,2,512,256]{3,2,1,0:T(8,128)(2,1)} %all-gather.5.cloned.1.call-done), kind=kLoop, calls=%fused_computation.24 | loop fusion | flops 2097152 | bytes 12582912 | tf_op jit(solution)/shard_map/convert_element_type | solution.py:76
  182.2 0.0 copy-done.6
  182.2 0.0 copy-done.7
  182.2 0.0 copy-start.8
  182.2 0.0 copy-start.9
  182.2 1.4 subtract_select_fusion
  183.6 0.1 copy-done.8
  183.8 0.6 copy-done.9
  184.4 27.5 %fusion.9 = f32[4,1024,256]{1,2,0:T(8,128)S(1)} fusion(f32[1024,1,512]{2,0,1:T(8,128)S(1)} %copy-done.8, f32[1024,1,512]{2,0,1:T(8,128)S(1)} %copy-done.9, f32[4,1,512,256]{3,2,1,0:T(8,128)S(1)} %get-tuple-element.18, f32[4,1,512,256]{3,2,1,0:T(8,128)S(1)} %get-tuple-element.19, f32[4,1,512,256]{3,2,1,0:T(8,128)S(1)} %get-tuple-element.6, ...), kind=kOutput, calls=%fused_computation.16 | convolution fusion | flops 12891193344 | bytes 16777224 | tf_op jit(solution)/shard_map/npk,spkc->snc/dot_general | solution.py:85
  211.9 0.0 copy-start.5
  211.9 1.7 slice.76
  213.6 1.0 copy-done.5
  214.7 1.4 collective-permute-start
  216.1 1.3 fusion.36
  217.3 1.6 copy.33
  218.9 44.5 %collective-permute-done = f32[4,512,256]{1,2,0:T(8,128)} collective-permute-done((f32[4,512,256]{1,2,0:T(8,128)}, f32[4,512,256]{1,2,0:T(8,128)}, u32[]{:S(2)}, u32[]{:S(2)}) %collective-permute-start) | collective-permute-done | bytes 2097184 | tf_op jit(solution)/shard_map/ppermute | solution.py:11
  263.5 0.0 copy-done.10
  263.5 4.0 %fusion.17 = bf16[4,512,256]{1,2,0:T(8,128)(2,1)} fusion(f32[4,512,256]{1,2,0:T(8,128)} %collective-permute-done, f32[4,1024,256]{1,2,0:T(8,128)} %copy-done.5, bf16[4,512,256]{1,2,0:T(8,128)(2,1)S(1)} %copy-done.4, bf16[4,512,1,256]{1,3,0,2:T(8,128)(2,1)S(1)} %copy.33, f32[256]{0:T(256)S(1)} %copy-done.10), kind=kLoop, calls=%fused_computation.23 | loop fusion | flops 3670016 | bytes 7341056 | tf_op jit(solution)/shard_map/convert_element_type | solution.py:90
  267.5 1.7 copy.27
  269.2 0.0 copy-start.1
  269.2 32.6 %all_to_all.23 = bf16[4,512,256]{2,0,1:T(4,128)(2,1)S(1)} all-to-all(bf16[4,512,256]{2,0,1:T(4,128)(2,1)S(1)} %copy.27), channel_id=1, replica_groups=mesh['ctx'=2,'ch'=16] {'ch'}, dimensions={1} | all-to-all | bytes 2097152 | tf_op jit(solution)/shard_map/all_to_all | solution.py:91
  301.8 0.1 copy.28
  301.9 1.1 copy.36
  (13 shorter events, 0.0 us)
Async XLA Ops:
  6.5 41.4 %copy-start = (f32[512,256]{1,0:T(8,128)S(1)}, f32[512,256]{1,0:T(8,128)}, u32[]{:S(2)}) copy-start(f32[512,256]{1,0:T(8,128)} %param.4) | copy-start | bytes 1572868
  32.5 74.4 %all-to-all-start = ((bf16[16,4,32,3,256]{4,2,3,1,0:T(8,128)(2,1)}), bf16[16,4,32,3,256]{4,2,3,1,0:T(8,128)(2,1)}, u32[]{:S(2)}, u32[]{:S(2)}) async-start(bf16[16,4,32,3,256]{4,2,3,1,0:T(8,128)(2,1)} %bitcast_dynamic-update-slice_fusion), calls=%async_computation | async-start | bytes 6291456 | tf_op jit(solution)/shard_map/all_to_all | solution.py:55
  39.1 99.9 %all-gather.7.cloned.1.call-start = ((), (), s32[]{:S(2)}) async-start(), calls=%async_computation.3 | async-start | bytes 3145728 | tf_op jit(solution)/shard_map/all_gather | solution.py:70
  43.0 4.0 %copy-start.2 = (f32[1,512,512]{2,1,0:T(8,128)}, f32[1,512,512]{2,1,0:T(8,128)S(1)}, u32[]{:S(2)}) copy-start(f32[1,512,512]{2,1,0:T(8,128)S(1)} %fusion.35) | copy-start | bytes 3145732
  47.0 1.0 copy-start.3
  50.8 128.2 %all-gather.5.cloned.1.call-start = ((), (), s32[]{:S(2)}) async-start(), calls=%async_computation.2 | async-start | bytes 6291456 | tf_op jit(solution)/shard_map/all_gather | solution.py:72
  178.9 3.2 %copy-start.6 = (f32[512,256]{1,0:T(8,128)S(1)}, f32[512,256]{1,0:T(8,128)}, u32[]{:S(2)}) copy-start(f32[512,256]{1,0:T(8,128)} %get-tuple-element.16) | copy-start | bytes 1572868
  178.9 3.2 %copy-start.7 = (f32[512,256]{1,0:T(8,128)S(1)}, f32[512,256]{1,0:T(8,128)}, u32[]{:S(2)}) copy-start(f32[512,256]{1,0:T(8,128)} %get-tuple-element.17) | copy-start | bytes 1572868
  182.2 1.6 copy-start.8
  182.2 2.2 copy-start.9
  211.9 2.7 copy-start.5
  214.7 48.8 %copy-start.10 = (f32[256]{0:T(256)S(1)}, f32[256]{0:T(256)}, u32[]{:S(2)}) copy-start(f32[256]{0:T(256)} %param.5) | copy-start | bytes 3076
  214.7 48.8 %collective-permute-start = (f32[4,512,256]{1,2,0:T(8,128)}, f32[4,512,256]{1,2,0:T(8,128)}, u32[]{:S(2)}, u32[]{:S(2)}) collective-permute-start(f32[4,512,256]{1,2,0:T(8,128)} %slice.76), channel_id=1, source_target_pairs={{0,16},{1,17},{2,18},{3,19},{4,20},{5,21},{6,22},{7,23},{8,24},{9,... | collective-permute-start | bytes 6291464 | tf_op jit(solution)/shard_map/ppermute | solution.py:11
  217.3 46.1 %copy-start.4 = (bf16[4,512,256]{1,2,0:T(8,128)(2,1)S(1)}, bf16[4,512,256]{1,2,0:T(8,128)(2,1)}, u32[]{:S(2)}) copy-start(bf16[4,512,256]{1,2,0:T(8,128)(2,1)} %fusion.36) | copy-start | bytes 3145732
  269.2 33.8 %copy-start.1 = (f32[512,256]{1,0:T(8,128)S(1)}, f32[512,256]{1,0:T(8,128)}, u32[]{:S(2)}) copy-start(f32[512,256]{1,0:T(8,128)} %param.4) | copy-start | bytes 1572868
Sparse Core Ops, SparseCore 0:
  50.9 32.7 all-gather.6
  121.5 57.4 all-gather.4
